TPU v7x, 32 devices: a whole 2x2x4 slice. The times are simulated.
32 devices in a mesh: tok: 8 (over y, x, core), head: 4 (over z).
Axes of the slice: x: 2, y: 2, z: 4, core: 2. Of those that a mesh axis runs over, the one named last changes fastest.
Arguments:
- pre_tokens: bfloat16 [8192, 2048], P('tok'), may hold values from -6 to 6
- dec_tokens: bfloat16 [16, 2048], P('tok'), may hold values from -6 to 6
- attn_gain: float32 [2048], replicated, may hold values from 0.1 to 1.9
- mlp_gain: float32 [2048], replicated, may hold values from 0.1 to 1.9
- w_qkv: bfloat16 [3, 2048, 2048], P(None, 'head', 'tok'), may hold values from -0.125 to 0.125
- w_out: bfloat16 [2048, 2048], P('tok', 'head'), may hold values from -0.125 to 0.125
- w_gate_up: bfloat16 [2, 8192, 2048], P(None, 'head', 'tok'), may hold values from -0.125 to 0.125
- w_down: bfloat16 [2048, 8192], P('tok', 'head'), may hold values from -0.0625 to 0.0625
- pre_cache: bfloat16 [8, 2, 2048, 2048], P('tok', None, None, 'head'), may hold values from -60 to 60
- dec_cache: bfloat16 [16, 2, 4096, 2048], P('tok', None, None, 'head'), may hold values from -60 to 60
- pre_order: int32 [8], replicated, may hold values from 0 to 7, each once
- dec_order: int32 [16], replicated, may hold values from 0 to 15, each once
- pre_offsets: int32 [8], P('tok'), may hold values from 2 to 2048, as said below
- dec_lengths: int32 [16], P('tok'), may hold values from 2 to 4096, as said below
Outputs:
- pre_out: bfloat16 [8192, 2048], P('tok')
- dec_out: bfloat16 [16, 2048], P('tok')
Inputs may be any that keep to these rules, and one draw needn't show every extreme that they name: `pre_order`: the prefill request at position k is handled with the caches of position k, which lie on index k of tok. `dec_order`: positions k of one index of tok are those with k // 2 equal to it. `pre_offsets`: some position reaches 2048. `dec_lengths`: some position reaches 4096.
All inputs are finite; a program needn't handle non-finite values.
Results may differ from a plain program's by a relative error of at most 0.013.
Values may be sent and summed in bfloat16 or wider, within the bound.
A program may use at most 192 MiB of HBM per device.

v0:
```python
import jax
import jax.numpy as jnp
from jax import lax
from jax.sharding import PartitionSpec as P

HD = 64
BLOCK = 512
rope_base = 130000.0
norm_eps = 1e-05
masked_score = -1e30


def rotate(values, positions):
    width = values.shape[-1]
    half = width // 2
    freqs = rope_base ** (-(jnp.arange(half, dtype=jnp.float32) * 2.0 / width))
    angles = positions.astype(jnp.float32)[:, None] * freqs[None, :]
    cosine = jnp.cos(angles)[:, None, :]
    sine = jnp.sin(angles)[:, None, :]
    first = values[..., :half]
    second = values[..., half:]
    return jnp.concatenate(
        [first * cosine - second * sine, second * cosine + first * sine], axis=-1
    )


def rms_norm(rows, gain):
    rows = rows.astype(jnp.float32)
    factor = lax.rsqrt(jnp.mean(rows * rows, axis=-1, keepdims=True) + norm_eps)
    return (rows * factor * gain).astype(jnp.bfloat16)


def fold_rows(inputs, weights):
    return jnp.einsum(
        "td,kcd->ktc",
        inputs,
        lax.all_gather(weights, "tok", axis=2, tiled=True),
        preferred_element_type=jnp.float32,
    )


def map_rows(inputs, weights):
    return jnp.einsum(
        "tc,dc->td",
        inputs,
        lax.all_gather(weights, "tok", axis=0, tiled=True),
        preferred_element_type=jnp.float32,
    )


def over_heads(partial_value):
    return lax.psum(partial_value.astype(jnp.bfloat16), "head").astype(jnp.float32)


def attend_local(query, keys_new, values_new, positions, self_mask, cache, limit):
    rows_q = query.shape[0]
    heads = query.shape[1] // HD
    scale = 1.0 / jnp.sqrt(jnp.float32(HD))
    q_rot = rotate(query.reshape(rows_q, heads, HD).astype(jnp.float32), positions).astype(
        jnp.bfloat16
    )
    k_rot = rotate(keys_new.reshape(rows_q, heads, HD).astype(jnp.float32), positions).astype(
        jnp.bfloat16
    )
    v_new = values_new.reshape(rows_q, heads, HD)
    scores = jnp.einsum("qhd,khd->hqk", q_rot, k_rot, preferred_element_type=jnp.float32) * scale
    scores = jnp.where(self_mask[None], scores, masked_score)
    top = jnp.max(scores, axis=-1)
    weights = jnp.exp(scores - top[..., None])
    total = jnp.sum(weights, axis=-1)
    mixed = jnp.einsum(
        "hqk,khd->hqd", weights.astype(jnp.bfloat16), v_new, preferred_element_type=jnp.float32
    )
    cached = cache.reshape(2, cache.shape[1], heads, HD)

    def one_block(index, state):
        top_now, total_now, mixed_now = state
        begin = index * BLOCK
        keys_block = lax.dynamic_slice_in_dim(cached[0], begin, BLOCK, 0)
        values_block = lax.dynamic_slice_in_dim(cached[1], begin, BLOCK, 0)
        block_scores = (
            jnp.einsum("qhd,khd->hqk", q_rot, keys_block, preferred_element_type=jnp.float32)
            * scale
        )
        live = begin + jnp.arange(BLOCK, dtype=jnp.int32) < limit
        block_scores = jnp.where(live[None, None, :], block_scores, masked_score)
        new_top = jnp.maximum(top_now, jnp.max(block_scores, axis=-1))
        factor = jnp.exp(top_now - new_top)
        block_weights = jnp.exp(block_scores - new_top[..., None])
        total_next = total_now * factor + jnp.sum(block_weights, axis=-1)
        mixed_next = mixed_now * factor[..., None] + jnp.einsum(
            "hqk,khd->hqd",
            block_weights.astype(jnp.bfloat16),
            values_block,
            preferred_element_type=jnp.float32,
        )
        return (new_top, total_next, mixed_next)

    block_count = cache.shape[1] // BLOCK
    top, total, mixed = lax.fori_loop(0, block_count, one_block, (top, total, mixed))
    result = mixed / total[..., None]
    return jnp.transpose(result, (1, 0, 2)).reshape(rows_q, heads * HD).astype(jnp.bfloat16)


def on_device(
    pre_tokens,
    dec_tokens,
    attn_gain,
    mlp_gain,
    w_qkv,
    w_out,
    w_gate_up,
    w_down,
    pre_cache,
    dec_cache,
    pre_order,
    dec_order,
    pre_offsets,
    dec_lengths,
):
    tok_count = lax.axis_size("tok")
    tok_index = lax.axis_index("tok")
    span_rows = pre_tokens.shape[0]
    piece_len = span_rows // tok_count
    dec_local = dec_tokens.shape[0]
    dec_total = dec_order.shape[0]
    group_width = w_qkv.shape[1]
    rows = jnp.concatenate([pre_tokens, dec_tokens], axis=0)
    normed = rms_norm(rows, attn_gain)
    projected = fold_rows(normed, w_qkv).astype(jnp.bfloat16)
    pre_part = projected[:, :span_rows].reshape(3, tok_count, piece_len, group_width)
    pre_send = jnp.take(pre_part, pre_order, axis=1)
    dec_part = projected[:, span_rows:]
    dec_send = jnp.broadcast_to(dec_part[:, None], (3, tok_count, dec_local, group_width))
    pre_recv, dec_recv = (
        lax.all_to_all(pre_send, "tok", split_axis=1, concat_axis=1, tiled=True),
        lax.all_to_all(dec_send, "tok", split_axis=1, concat_axis=1, tiled=True),
    )
    pre_recv = pre_recv.reshape(3, span_rows, group_width)
    dec_recv = dec_recv.reshape(3, dec_total, group_width)
    offset_now = pre_offsets[0]
    pre_positions = offset_now + jnp.arange(span_rows, dtype=jnp.int32)
    causal = (
        jnp.arange(span_rows, dtype=jnp.int32)[None, :]
        <= jnp.arange(span_rows, dtype=jnp.int32)[:, None]
    )
    pre_att = attend_local(
        pre_recv[0], pre_recv[1], pre_recv[2], pre_positions, causal, pre_cache[0], offset_now
    )
    own_slots = lax.dynamic_slice_in_dim(dec_order, tok_index * dec_local, dec_local)
    dec_mine = jnp.take(dec_recv, own_slots, axis=1)
    self_only = jnp.ones((1, 1), jnp.bool_)
    dec_results = []
    for request in range(dec_local):
        length_now = dec_lengths[request]
        dec_results.append(
            attend_local(
                dec_mine[0, request : request + 1],
                dec_mine[1, request : request + 1],
                dec_mine[2, request : request + 1],
                dec_lengths[request : request + 1],
                self_only,
                dec_cache[request],
                length_now,
            )
        )
    dec_att = jnp.concatenate(dec_results, axis=0)
    picker = (jnp.arange(dec_total, dtype=jnp.int32)[:, None] == own_slots[None, :]).astype(
        jnp.bfloat16
    )
    dec_back = (
        jnp.dot(picker, dec_att, preferred_element_type=jnp.float32)
        .astype(jnp.bfloat16)
        .reshape(tok_count, dec_local, group_width)
    )
    pre_back = pre_att.reshape(tok_count, piece_len, group_width)
    pre_ret, dec_ret = (
        lax.all_to_all(pre_back, "tok", split_axis=0, concat_axis=0, tiled=True),
        lax.all_to_all(dec_back, "tok", split_axis=0, concat_axis=0, tiled=True),
    )
    slot_range = jnp.arange(tok_count, dtype=jnp.int32)
    inverse = jnp.sum(
        jnp.where(pre_order[None, :] == slot_range[:, None], slot_range[None, :], 0), axis=1
    )
    pre_mixed = jnp.take(pre_ret, inverse, axis=0).reshape(span_rows, group_width)
    dec_mixed = jnp.sum(dec_ret.astype(jnp.float32), axis=0).astype(jnp.bfloat16)
    attended = jnp.concatenate([pre_mixed, dec_mixed], axis=0)
    resid = rows.astype(jnp.float32) + over_heads(map_rows(attended, w_out))
    mlp_in = rms_norm(resid, mlp_gain)
    gate_up = fold_rows(mlp_in, w_gate_up)
    hidden = (jax.nn.silu(gate_up[0]) * gate_up[1]).astype(jnp.bfloat16)
    final = (resid + over_heads(map_rows(hidden, w_down))).astype(jnp.bfloat16)
    return (final[:span_rows], final[span_rows:])


def solution(mesh):
    placed = (
        P("tok", None),
        P("tok", None),
        P(),
        P(),
        P(None, "head", "tok"),
        P("tok", "head"),
        P(None, "head", "tok"),
        P("tok", "head"),
        P("tok", None, None, "head"),
        P("tok", None, None, "head"),
        P(),
        P(),
        P("tok"),
        P("tok"),
    )
    return jax.shard_map(
        on_device,
        mesh=mesh,
        in_specs=placed,
        out_specs=(P("tok", None), P("tok", None)),
        check_vma=False,
    )
```

profile of v0, /device:TPU:0, one launch (start us, length us, event | category | flops | bytes accessed | tf_op | source)
XLA Modules:
  0.0 917.4 jit_solution(6938060684797594388)
XLA Ops:
  22.7 11.3 %fusion.97 = (bf16[1,2,4096,512]{3,2,1,0:T(8,128)(2,1)}, bf16[1,2,4096,512]{3,2,1,0:T(8,128)(2,1)}) fusion(bf16[2,2,4096,512]{3,2,1,0:T(8,128)(2,1)} %param.29), kind=kLoop, calls=%fused_computation.196 | loop fusion | bytes 33554432 | tf_op jit(solution)/shard_map/slice | solution.py:163
  34.1 11.3 %copy.94 = bf16[1,2,4096,512]{2,3,1,0:T(8,128)(2,1)} copy(bf16[1,2,4096,512]{3,2,1,0:T(8,128)(2,1)} %get-tuple-element.511) | data formatting | bytes 16777216
  45.4 18.9 %copy.67 = bf16[2,4096,8,64]{3,2,1,0:T(8,128)(2,1)} copy(bf16[2,4096,8,64]{1,3,2,0:T(8,128)(2,1)} %bitcast.220) | data formatting | bytes 16777216 | tf_op jit(solution)/shard_map/while | solution.py:100
  64.9 11.7 %copy.95 = bf16[1,2,4096,512]{2,3,1,0:T(8,128)(2,1)} copy(bf16[1,2,4096,512]{3,2,1,0:T(8,128)(2,1)} %get-tuple-element.512) | data formatting | bytes 16777216
  76.6 19.0 %copy.69 = bf16[2,4096,8,64]{3,2,1,0:T(8,128)(2,1)} copy(bf16[2,4096,8,64]{1,3,2,0:T(8,128)(2,1)} %bitcast.221) | data formatting | bytes 16777216 | tf_op jit(solution)/shard_map/while | solution.py:100
  96.2 10.4 %fusion.59 = bf16[3,1026,512]{2,1,0:T(8,128)(2,1)S(1)} fusion(bf16[3,512,2048]{2,1,0:T(8,128)(2,1)} %all-gather.5.cloned.1.call-done, f32[2048]{0:T(1024)S(1)} %copy-done.10, f32[1026]{0:T(1024)S(1)} %add_rsqrt_fusion.1, bf16[2,2048]{1,0:T(2,128)(2,1)S(1)} %copy-done.4, bf16[1024,2048]{1,0:T(8,128)(2,1)} %param.20), kind=kOutput, calls=%fused_computation.96 | convolution fusion | flops 6471318528 | bytes 13658120 | tf_op jit(solution)/shard_map/td,kcd->ktc/dot_general | solution.py:34
  125.0 66.9 %while.52 = (s32[]{:T(128)}, f32[8,1]{0,1:T(1,128)S(1)}, f32[8,1]{0,1:T(1,128)S(1)}, f32[8,1,64]{2,1,0:T(1,128)S(1)}, s32[]{:T(128)}, /*index=5*/bf16[2,4096,8,6...) while((s32[]{:T(128)}, f32[8,1]{0,1:T(1,128)S(1)}, ...), condition=%wide.region_11.12_spmd, body=%wide.region_8.11_spmd.sunk | while | flops 1083422 | bytes 19995780 | solution.py:100
  125.0 6.5 fusion.138
  133.3 6.5 fusion.138
  141.7 6.5 fusion.138
  150.1 6.5 fusion.138
  158.4 6.5 fusion.138
  166.8 6.5 fusion.138
  175.2 6.5 fusion.138
  183.5 6.5 fusion.138
  192.5 66.4 %while.53 = (s32[]{:T(128)}, f32[8,1]{0,1:T(1,128)S(1)}, f32[8,1]{0,1:T(1,128)S(1)}, f32[8,1,64]{2,1,0:T(1,128)S(1)}, s32[]{:T(128)}, /*index=5*/bf16[2,4096,8,6...) while((s32[]{:T(128)}, f32[8,1]{0,1:T(1,128)S(1)}, ...), condition=%wide.region_15.16_spmd, body=%wide.region_12.15_spmd.sunk | while | flops 1083422 | bytes 19995780 | solution.py:100
  192.5 6.5 fusion.147
  200.8 6.5 fusion.147
  209.1 6.5 fusion.147
  217.4 6.5 fusion.147
  225.7 6.5 fusion.147
  284.8 13.6 %fusion.39 = (f32[8,1024]{1,0:T(8,128)S(1)}, f32[8,1024,1024]{1,2,0:T(8,128)}) fusion(pred[1024,1024]{0,1:T(8,128)(4,1)S(1)} %copy-done, bf16[1024,8,32]{0,2,1:T(8,128)(2,1)S(1)} %get-tuple-element.520, bf16[1024,8,32]{0,2,1:T(8,128)(2,1)S(1)} %get-tuple-element.521, bf16[1024,8,32]{0,2,1:T(8,128)(2,1)S(1)} %get-tuple-element.517, ...), kind=kOutput, calls=%fused_computation.66 | convolution fusion | flops 1103093760 | bytes 36732928 | tf_op jit(solution)/shard_map/qhd,khd->hqk/dot_general | solution.py:66
  298.4 14.3 %fusion.41 = f32[8,1024]{1,0:T(8,128)S(1)} fusion(f32[8,1024,1024]{1,2,0:T(8,128)} %get-tuple-element.545, f32[8,1024]{1,0:T(8,128)S(1)} %get-tuple-element.790, pred[1024,1024]{0,1:T(8,128)(4,1)S(1)} %copy-done), kind=kLoop, calls=%fused_computation.68 | loop fusion | flops 33546240 | bytes 34668544 | tf_op jit(solution)/shard_map/reduce_sum | solution.py:70
  312.7 16.0 %fusion.42 = f32[8,1024,64]{1,2,0:T(8,128)} fusion(bf16[1024,8,64]{0,2,1:T(8,128)(2,1)S(1)} %copy-done.3, f32[8,1024,1024]{1,2,0:T(8,128)} %get-tuple-element.545, f32[8,1024]{1,0:T(8,128)S(1)} %get-tuple-element.790, pred[1024,1024]{0,1:T(8,128)(4,1)S(1)} %copy-done), kind=kOutput, calls=%fused_computation.69 | convolution fusion | flops 1107296256 | bytes 37781504 | tf_op jit(solution)/shard_map/hqk,khd->hqd/dot_general | solution.py:71
  328.8 63.3 %while.51 = (s32[]{:T(128)}, f32[8,1024]{1,0:T(8,128)S(1)}, f32[8,1024]{1,0:T(8,128)S(1)}, f32[8,1024,64]{1,2,0:T(8,128)}, s32[]{:T(128)}, /*index=5*/bf16[2,204...) while((s32[]{:T(128)}, f32[8,1024]{1,0:T(8,128)S(1)}, ...), condition=%wide.region_7.8_spmd, body=%wide.region_4.7_spmd.sunk | while | flops 1120945152 | bytes 82315496 | solution.py:100
  400.9 14.4 %all-to-all-done.1 = bf16[8,128,512]{2,1,0:T(8,128)(2,1)S(1)} async-done(((bf16[8,128,512]{2,1,0:T(8,128)(2,1)}), bf16[8,128,512]{2,1,0:T(8,128)(2,1)S(1)}, u32[]{:S(2)}, u32[]{:S(2)}) %all-to-all-start.1) | async-done | bytes 1048608 | tf_op jit(solution)/shard_map/all_to_all | solution.py:178
  423.4 153.9 %all-reduce.3.cloned.1.call-done = bf16[1026,2048]{1,0:T(8,128)(2,1)} async-done(((bf16[1026,2048]{1,0:T(8,128)(2,1)}), bf16[1026,2048]{1,0:T(8,128)(2,1)}) %all-reduce.3.cloned.1.call-update) | async-done | bytes 4202512 | tf_op jit(solution)/shard_map/psum | solution.py:52
  581.7 89.4 %all-gather.9.cloned.1.call-done = bf16[2,2048,2048]{2,1,0:T(8,128)(2,1)} async-done(((bf16[2,2048,256]{2,1,0:T(8,128)(2,1)}), bf16[2,2048,2048]{2,1,0:T(8,128)(2,1)}) %all-gather.9.cloned.1.call-update) | async-done | bytes 16777232 | tf_op jit(solution)/shard_map/all_gather | solution.py:37
  671.2 25.3 %convolution_bitcast_fusion = f32[2,1026,2048]{2,1,0:T(8,128)} fusion(bf16[2,2048,2048]{2,1,0:T(8,128)(2,1)} %all-gather.9.cloned.1.call-done, bf16[1026,2048]{1,0:T(8,128)(2,1)} %all-reduce.3.cloned.1.call-done, f32[2048]{0:T(1024)S(1)} %copy-done.11, f32[1026]{0:T(1024)S(1)} %add_rsqrt_fusion, bf16[2,2048]{1,0:T(2,128)(2,1)S(1)} %copy-done.5, ...), kind=kOutput, calls=%fused_computation.71 | convolution fusion | flops 17232334848 | bytes 42004488 | tf_op jit(solution)/shard_map/td,kcd->ktc/dot_general | solution.py:34
  696.5 30.8 %all-gather.11.cloned.1.call-done = bf16[2048,2048]{1,0:T(8,128)(2,1)} async-done(((bf16[256,2048]{1,0:T(8,128)(2,1)}), bf16[2048,2048]{1,0:T(8,128)(2,1)}) %all-gather.11.cloned.1.call-update) | async-done | bytes 8388624 | tf_op jit(solution)/shard_map/all_gather | solution.py:46
  727.3 17.7 %convolution_convert_fusion = bf16[1026,2048]{1,0:T(8,128)(2,1)} fusion(bf16[2048,2048]{1,0:T(8,128)(2,1)} %all-gather.11.cloned.1.call-done, f32[2,1026,2048]{2,1,0:T(8,128)} %convolution_bitcast_fusion), kind=kOutput, calls=%fused_computation.85 | convolution fusion | flops 8621420544 | bytes 29401088 | tf_op jit(solution)/shard_map/tc,dc->td/dot_general | solution.py:43
  745.0 156.2 %all-reduce.5.cloned.1.call-done = bf16[1026,2048]{1,0:T(8,128)(2,1)} async-done(((bf16[1026,2048]{1,0:T(8,128)(2,1)}), bf16[1026,2048]{1,0:T(8,128)(2,1)}) %all-reduce.5.cloned.1.call-update) | async-done | bytes 4202512 | tf_op jit(solution)/shard_map/psum | solution.py:52
  (311 shorter events, 200.9 us)
Async XLA Ops:
  7.2 14.2 %copy-start.9 = (s32[16]{0:T(128)S(1)}, s32[16]{0:T(128)}, u32[]{:S(2)}) copy-start(s32[16]{0:T(128)} %param.31) | copy-start | bytes 196
  7.2 14.3 %copy-start.6 = (s32[2]{0:T(128)S(1)}, s32[2]{0:T(128)}, u32[]{:S(2)}) copy-start(s32[2]{0:T(128)} %param.33) | copy-start | bytes 28
  7.2 89.0 %all-gather.5.cloned.1.call-start = ((), (), s32[]{:S(2)}) async-start(), calls=%async_computation.4 | async-start | bytes 7077888 | tf_op jit(solution)/shard_map/all_gather | solution.py:37
  7.9 408.3 %all-gather.7.cloned.1.call-start = ((), (), s32[]{:S(2)}) async-start(), calls=%async_computation.5 | async-start | bytes 2359296 | tf_op jit(solution)/shard_map/all_gather | solution.py:46
  21.5 12.6 %copy-start.7 = (s32[2]{0:T(128)}, s32[2]{0:T(128)S(1)}, u32[]{:S(2)}) copy-start(s32[2]{0:T(128)S(1)} %get-tuple-element.494) | copy-start | bytes 28
  76.6 19.5 %copy-start.4 = (bf16[2,2048]{1,0:T(2,128)(2,1)S(1)}, bf16[2,2048]{1,0:T(2,128)(2,1)}, u32[]{:S(2)}) copy-start(bf16[2,2048]{1,0:T(2,128)(2,1)} %param.21) | copy-start | bytes 24580
  76.6 19.6 %copy-start.10 = (f32[2048]{0:T(1024)S(1)}, f32[2048]{0:T(1024)}, u32[]{:S(2)}) copy-start(f32[2048]{0:T(1024)} %param.22) | copy-start | bytes 24580
  107.5 11.9 %all-to-all-start.2 = ((bf16[3,8,2,512]{3,2,0,1:T(2,128)(2,1)}), bf16[3,8,2,512]{3,2,0,1:T(2,128)(2,1)S(1)}, u32[]{:S(2)}, u32[]{:S(2)}) async-start(bf16[3,8,2,512]{3,2,0,1:T(2,128)(2,1)} %broadcast_in_dim.223), calls=%async_computation.2 | async-start | bytes 98304 | tf_op jit(solution)/shard_map/all_to_all | solution.py:137
  119.4 140.7 %all-to-all-start = ((bf16[3,8,128,512]{3,2,0,1:T(8,128)(2,1)}), bf16[3,8,128,512]{3,2,0,1:T(8,128)(2,1)S(1)}, u32[]{:S(2)}, u32[]{:S(2)}) async-start(bf16[3,8,128,512]{3,2,0,1:T(8,128)(2,1)} %select_bitcast_fusion), calls=%async_computation | async-start | bytes 6291456 | tf_op jit(solution)/shard_map/all_to_all | solution.py:136
  192.5 66.8 %copy-start.8 = (s32[2]{0:T(128)S(1)}, s32[2]{0:T(128)}, u32[]{:S(2)}) copy-start(s32[2]{0:T(128)} %copy-done.7) | copy-start | bytes 28
  260.0 135.7 %all-to-all-start.3 = ((bf16[8,2,512]{2,1,0:T(2,128)(2,1)}), bf16[8,2,512]{2,1,0:T(2,128)(2,1)}, u32[]{:S(2)}, u32[]{:S(2)}) async-start(bf16[8,2,512]{2,1,0:T(2,128)(2,1)} %reshape.531), calls=%async_computation.3 | async-start | bytes 32768 | tf_op jit(solution)/shard_map/all_to_all | solution.py:179
  275.0 9.9 %copy-start = (pred[1024,1024]{0,1:T(8,128)(4,1)S(1)}, pred[1024,1024]{0,1:T(8,128)(4,1)}, u32[]{:S(2)}) copy-start(pred[1024,1024]{0,1:T(8,128)(4,1)} %iota_compare_fusion) | copy-start | bytes 3145732
  298.4 14.3 %copy-start.3 = (bf16[1024,8,64]{0,2,1:T(8,128)(2,1)S(1)}, bf16[1024,8,64]{0,2,1:T(8,128)(2,1)}, u32[]{:S(2)}) copy-start(bf16[1024,8,64]{0,2,1:T(8,128)(2,1)} %reshape_squeeze.8) | copy-start | bytes 3145732
  335.6 3.9 copy-start.1
  343.4 1.3 copy-start.2
  351.4 3.9 copy-start.1
  359.2 1.3 copy-start.2
  367.1 3.9 copy-start.1
  375.0 1.3 copy-start.2
  382.9 3.9 copy-start.1
  390.8 1.3 copy-start.2
  392.1 7.9 copy-start.12
  395.7 19.6 %all-to-all-start.1 = ((bf16[8,128,512]{2,1,0:T(8,128)(2,1)}), bf16[8,128,512]{2,1,0:T(8,128)(2,1)S(1)}, u32[]{:S(2)}, u32[]{:S(2)}) async-start(bf16[8,128,512]{2,1,0:T(8,128)(2,1)} %copy.64), calls=%async_computation.1 | async-start | bytes 2097152 | tf_op jit(solution)/shard_map/all_to_all | solution.py:178
  399.9 177.3 %all-reduce.3.cloned.1.call-start = ((), (), s32[]{:S(2)}) async-start(), calls=%async_computation.6 | async-start | bytes 8454144 | tf_op jit(solution)/shard_map/psum | solution.py:52
  416.2 161.1 %copy-start.5 = (bf16[2,2048]{1,0:T(2,128)(2,1)S(1)}, bf16[2,2048]{1,0:T(2,128)(2,1)}, u32[]{:S(2)}) copy-start(bf16[2,2048]{1,0:T(2,128)(2,1)} %param.21) | copy-start | bytes 24580
  422.2 249.0 %copy-start.11 = (f32[2048]{0:T(1024)S(1)}, f32[2048]{0:T(1024)}, u32[]{:S(2)}) copy-start(f32[2048]{0:T(1024)} %param.23) | copy-start | bytes 24580
  422.2 249.0 %all-gather.9.cloned.1.call-start = ((), (), s32[]{:S(2)}) async-start(), calls=%async_computation.7 | async-start | bytes 18874368 | tf_op jit(solution)/shard_map/all_gather | solution.py:37
  422.8 304.6 %all-gather.11.cloned.1.call-start = ((), (), s32[]{:S(2)}) async-start(), calls=%async_computation.8 | async-start | bytes 9437184 | tf_op jit(solution)/shard_map/all_gather | solution.py:46
  423.4 477.9 %all-reduce.5.cloned.1.call-start = ((), (), s32[]{:S(2)}) async-start(), calls=%async_computation.9 | async-start | bytes 8454144 | tf_op jit(solution)/shard_map/psum | solution.py:52
Sparse Core Ops, SparseCore 0:
  9.9 49.3 all-gather.4
  61.2 27.9 all-gather.6
  422.3 154.9 all-reduce.2
  579.0 92.1 all-gather.8
  672.9 54.3 all-gather.10
  745.2 156.0 all-reduce.4
where the time goes:
time: 928 us; the launch traced here: 917 us
  waiting for transfers between devices  447 us (48%)
  local copies, waits for them, and re-layouts  227 us (24%)
  matrix products  129 us (14%)
  other arithmetic  77.7 us (8%)
  starting transfers between devices  19 us (2%)
  between operations  16.5 us (2%)
    psum x2, waiting for transfers between devices, over_heads(): lax.psum(partial_value.astype(jnp.bfloat16), 'head').astype(jnp.float32)  310 us
    slice x20, local copies, waits for them, and re-layouts, one_block(): values_block = lax.dynamic_slice_in_dim(cached[1], begin, BLOCK, 0)  115 us
    all_gather x2, waiting for transfers between devices, fold_rows(): lax.all_gather(weights, 'tok', axis=2, tiled=True)  89.5 us
    while x2, local copies, waits for them, and re-layouts, attend_local(): lax.fori_loop(0, block_count, one_block, (top, total, mixed))  37.9 us
    dot_general x2, matrix products, fold_rows(): jnp.einsum('td,kcd->ktc', inputs, lax.all_gather(weights, 'tok', axis=2,...  35.7 us
    all_gather x2, waiting for transfers between devices, map_rows(): lax.all_gather(weights, 'tok', axis=0, tiled=True)  30.8 us
    unnamed x26, local copies, waits for them, and re-layouts  29.5 us
    dot_general x2, matrix products, map_rows(): jnp.einsum('tc,dc->td', inputs, lax.all_gather(weights, 'tok', axis=0, ti...  23.6 us
  transfers between devices with their start and end apart: 10, of which 5 were waited for; matrix products, arithmetic and copies ran while one was open for 43% of the time, Pallas kernels for 0%

commit v1 on v0

--- a/solution.py
+++ b/solution.py
@@ -8,6 +8,12 @@
 rope_base = 130000.0
 norm_eps = 1e-05
 masked_score = -1e30
+
+
+def summed_here(block, name):
+    pieces = lax.all_gather(block, name, axis=0, tiled=False)
+    total = pieces.sum(axis=0)
+    return total
 
 
 def rotate(values, positions):
@@ -49,7 +55,7 @@
 
 
 def over_heads(partial_value):
-    return lax.psum(partial_value.astype(jnp.bfloat16), "head").astype(jnp.float32)
+    return summed_here(partial_value.astype(jnp.bfloat16), "head").astype(jnp.float32)
 
 
 def attend_local(query, keys_new, values_new, positions, self_mask, cache, limit):

time: 928 us -> 1210 us (1.30)
  waiting for transfers between devices: 447 us -> 703 us
  other arithmetic: 77.7 us -> 103 us
    all_gather x0 -> x2, waiting for transfers between devices: none -> 579 us  [summed_here(): pieces = lax.all_gather(block, name, axis=0, tiled=False)]
    psum x2 -> x0, waiting for transfers between devices: 310 us -> none  [over_heads(): lax.psum(partial_value.astype(jnp.bfloat16), 'head').astype(jnp.float32)]
    reduce_sum x0 -> x2, other arithmetic: none -> 24.6 us  [summed_here(): total = pieces.sum(axis=0)]
    all_gather x2, waiting for transfers between devices: 89.5 us -> 76.8 us  [fold_rows(): lax.all_gather(weights, 'tok', axis=2, tiled=True)]
  transfers between devices with their start and end apart: 10 -> 10, of which waited for: 5 -> 5; matrix products, arithmetic and copies ran while one was open for 43% -> 34% of each run, Pallas kernels for 0% -> 0%
where the time goes in v1:
time: 1210 us; the launch traced here: 1200 us
  waiting for transfers between devices  703 us (58%)
  local copies, waits for them, and re-layouts  227 us (19%)
  matrix products  129 us (11%)
  other arithmetic  103 us (9%)
  starting transfers between devices  19.2 us (2%)
  between operations  16.5 us (1%)
    all_gather x2, waiting for transfers between devices, summed_here(): pieces = lax.all_gather(block, name, axis=0, tiled=False)  579 us
    slice x20, local copies, waits for them, and re-layouts, one_block(): values_block = lax.dynamic_slice_in_dim(cached[1], begin, BLOCK, 0)  115 us
    all_gather x2, waiting for transfers between devices, fold_rows(): lax.all_gather(weights, 'tok', axis=2, tiled=True)  76.8 us
    while x2, local copies, waits for them, and re-layouts, attend_local(): lax.fori_loop(0, block_count, one_block, (top, total, mixed))  37.9 us
    dot_general x2, matrix products, fold_rows(): jnp.einsum('td,kcd->ktc', inputs, lax.all_gather(weights, 'tok', axis=2,...  35.7 us
    all_gather x2, waiting for transfers between devices, map_rows(): lax.all_gather(weights, 'tok', axis=0, tiled=True)  30.9 us
    unnamed x26, local copies, waits for them, and re-layouts  29.5 us
    reduce_sum x2, other arithmetic, summed_here(): total = pieces.sum(axis=0)  24.6 us
  transfers between devices with their start and end apart: 10, of which 5 were waited for; matrix products, arithmetic and copies ran while one was open for 34% of the time, Pallas kernels for 0%

profile of v1, /device:TPU:0, one launch (start us, length us, event | category | flops | bytes accessed | tf_op | source)
XLA Modules:
  0.0 1198.5 jit_solution(6277692567860076559)
XLA Ops:
  22.7 11.3 fusion.99
  34.1 11.3 copy.94
  45.4 18.9 %copy.67 = bf16[2,4096,8,64]{3,2,1,0:T(8,128)(2,1)} copy(bf16[2,4096,8,64]{1,3,2,0:T(8,128)(2,1)} %bitcast.224) | data formatting | bytes 16777216 | tf_op jit(solution)/shard_map/while | solution.py:106
  64.9 11.7 copy.95
  76.6 19.0 %copy.69 = bf16[2,4096,8,64]{3,2,1,0:T(8,128)(2,1)} copy(bf16[2,4096,8,64]{1,3,2,0:T(8,128)(2,1)} %bitcast.225) | data formatting | bytes 16777216 | tf_op jit(solution)/shard_map/while | solution.py:106
  96.2 10.4 fusion.61
  125.0 66.9 %while.52 = (s32[]{:T(128)}, f32[8,1]{0,1:T(1,128)S(1)}, f32[8,1]{0,1:T(1,128)S(1)}, f32[8,1,64]{2,1,0:T(1,128)S(1)}, s32[]{:T(128)}, /*index=5*/bf16[2,4096,8,6...) while((s32[]{:T(128)}, f32[8,1]{0,1:T(1,128)S(1)}, ...), condition=%wide.region_11.12_spmd, body=%wide.region_8.11_spmd.sunk | while | flops 1083422 | bytes 19995780 | solution.py:106
  125.0 6.5 fusion.140
  133.3 6.5 fusion.140
  141.7 6.5 fusion.140
  150.1 6.5 fusion.140
  158.4 6.5 fusion.140
  166.8 6.5 fusion.140
  175.2 6.5 fusion.140
  183.5 6.5 fusion.140
  192.5 66.4 %while.53 = (s32[]{:T(128)}, f32[8,1]{0,1:T(1,128)S(1)}, f32[8,1]{0,1:T(1,128)S(1)}, f32[8,1,64]{2,1,0:T(1,128)S(1)}, s32[]{:T(128)}, /*index=5*/bf16[2,4096,8,6...) while((s32[]{:T(128)}, f32[8,1]{0,1:T(1,128)S(1)}, ...), condition=%wide.region_15.16_spmd, body=%wide.region_12.15_spmd.sunk | while | flops 1083422 | bytes 19995780 | solution.py:106
  192.5 6.5 fusion.149
  200.8 6.5 fusion.149
  209.1 6.5 fusion.149
  284.8 13.6 %fusion.39 = (f32[8,1024]{1,0:T(8,128)S(1)}, f32[8,1024,1024]{1,2,0:T(8,128)}) fusion(pred[1024,1024]{0,1:T(8,128)(4,1)S(1)} %copy-done, bf16[1024,8,32]{0,2,1:T(8,128)(2,1)S(1)} %get-tuple-element.520, bf16[1024,8,32]{0,2,1:T(8,128)(2,1)S(1)} %get-tuple-element.521, bf16[1024,8,32]{0,2,1:T(8,128)(2,1)S(1)} %get-tuple-element.517, ...), kind=kOutput, calls=%fused_computation.66 | convolution fusion | flops 1103093760 | bytes 36732928 | tf_op jit(solution)/shard_map/qhd,khd->hqk/dot_general | solution.py:72
  298.4 14.3 %fusion.41 = f32[8,1024]{1,0:T(8,128)S(1)} fusion(f32[8,1024,1024]{1,2,0:T(8,128)} %get-tuple-element.545, f32[8,1024]{1,0:T(8,128)S(1)} %get-tuple-element.790, pred[1024,1024]{0,1:T(8,128)(4,1)S(1)} %copy-done), kind=kLoop, calls=%fused_computation.68 | loop fusion | flops 33546240 | bytes 34668544 | tf_op jit(solution)/shard_map/reduce_sum | solution.py:76
  312.7 16.0 %fusion.42 = f32[8,1024,64]{1,2,0:T(8,128)} fusion(bf16[1024,8,64]{0,2,1:T(8,128)(2,1)S(1)} %copy-done.3, f32[8,1024,1024]{1,2,0:T(8,128)} %get-tuple-element.545, f32[8,1024]{1,0:T(8,128)S(1)} %get-tuple-element.790, pred[1024,1024]{0,1:T(8,128)(4,1)S(1)} %copy-done), kind=kOutput, calls=%fused_computation.69 | convolution fusion | flops 1107296256 | bytes 37781504 | tf_op jit(solution)/shard_map/hqk,khd->hqd/dot_general | solution.py:77
  328.8 63.3 %while.51 = (s32[]{:T(128)}, f32[8,1024]{1,0:T(8,128)S(1)}, f32[8,1024]{1,0:T(8,128)S(1)}, f32[8,1024,64]{1,2,0:T(8,128)}, s32[]{:T(128)}, /*index=5*/bf16[2,204...) while((s32[]{:T(128)}, f32[8,1024]{1,0:T(8,128)S(1)}, ...), condition=%wide.region_7.8_spmd, body=%wide.region_4.7_spmd.sunk | while | flops 1120945152 | bytes 82315496 | solution.py:106
  400.9 14.4 %all-to-all-done.1 = bf16[8,128,512]{2,1,0:T(8,128)(2,1)S(1)} async-done(((bf16[8,128,512]{2,1,0:T(8,128)(2,1)}), bf16[8,128,512]{2,1,0:T(8,128)(2,1)S(1)}, u32[]{:S(2)}, u32[]{:S(2)}) %all-to-all-start.1) | async-done | bytes 1048608 | tf_op jit(solution)/shard_map/all_to_all | solution.py:184
  423.6 288.1 %all-gather.19.cloned.1.call-done = bf16[4,1026,2048]{2,1,0:T(8,128)(2,1)} async-done(((bf16[1,1026,2048]{2,1,0:T(8,128)(2,1)}), bf16[4,1026,2048]{2,1,0:T(8,128)(2,1)}) %all-gather.19.cloned.1.call-update) | async-done | bytes 16810000 | tf_op jit(solution)/shard_map/all_gather | solution.py:14
  711.7 12.6 %reduce_sum.132 = bf16[1026,2048]{1,0:T(8,128)(2,1)} reduce(bf16[4,1026,2048]{2,1,0:T(8,128)(2,1)} %all-gather.19.cloned.1.call-done, bf16[]{:T(256)} %constant.259.clone.1), dimensions={0}, to_apply=%region_17.18 | reduce | flops 6303744 | bytes 21012482 | tf_op jit(solution)/shard_map/reduce_sum | solution.py:15
  728.9 76.8 %all-gather.15.cloned.1.call-done = bf16[2,2048,2048]{2,1,0:T(8,128)(2,1)} async-done(((bf16[2,2048,256]{2,1,0:T(8,128)(2,1)}), bf16[2,2048,2048]{2,1,0:T(8,128)(2,1)}) %all-gather.15.cloned.1.call-update) | async-done | bytes 16777232 | tf_op jit(solution)/shard_map/all_gather | solution.py:43
  805.7 25.3 %convolution_bitcast_fusion = f32[2,1026,2048]{2,1,0:T(8,128)} fusion(bf16[2,2048,2048]{2,1,0:T(8,128)(2,1)} %all-gather.15.cloned.1.call-done, bf16[1026,2048]{1,0:T(8,128)(2,1)} %reduce_sum.132, f32[2048]{0:T(1024)S(1)} %copy-done.11, f32[1026]{0:T(1024)S(1)} %add_rsqrt_fusion, bf16[2,2048]{1,0:T(2,128)(2,1)S(1)} %copy-done.5, bf16[1024,2048]{1,0:T(8,128)(2,1)} %param.20), kind=kOutput, calls=%fused_computation.71 | convolution fusion | flops 17232334848 | bytes 42004488 | tf_op jit(solution)/shard_map/td,kcd->ktc/dot_general | solution.py:40
  831.0 30.8 %all-gather.17.cloned.1.call-done = bf16[2048,2048]{1,0:T(8,128)(2,1)} async-done(((bf16[256,2048]{1,0:T(8,128)(2,1)}), bf16[2048,2048]{1,0:T(8,128)(2,1)}) %all-gather.17.cloned.1.call-update) | async-done | bytes 8388624 | tf_op jit(solution)/shard_map/all_gather | solution.py:52
  861.8 17.7 %fusion.51 = bf16[1,1026,2048]{2,1,0:T(8,128)(2,1)} fusion(bf16[2048,2048]{1,0:T(8,128)(2,1)} %all-gather.17.cloned.1.call-done, f32[2,1026,2048]{2,1,0:T(8,128)} %convolution_bitcast_fusion), kind=kOutput, calls=%fused_computation.88 | convolution fusion | flops 8621420544 | bytes 29401088 | tf_op jit(solution)/shard_map/tc,dc->td/dot_general | solution.py:49
  879.6 290.7 %all-gather.21.cloned.1.call-done = bf16[4,1026,2048]{2,1,0:T(8,128)(2,1)} async-done(((bf16[1,1026,2048]{2,1,0:T(8,128)(2,1)}), bf16[4,1026,2048]{2,1,0:T(8,128)(2,1)}) %all-gather.21.cloned.1.call-update) | async-done | bytes 16810000 | tf_op jit(solution)/shard_map/all_gather | solution.py:14
  1170.2 12.1 %reduce_sum.134 = bf16[1026,2048]{1,0:T(8,128)(2,1)} reduce(bf16[4,1026,2048]{2,1,0:T(8,128)(2,1)} %all-gather.21.cloned.1.call-done, bf16[]{:T(256)} %constant.259.clone.1), dimensions={0}, to_apply=%region_19.20 | reduce | flops 6303744 | bytes 21012482 | tf_op jit(solution)/shard_map/reduce_sum | solution.py:15
  (313 shorter events, 214.3 us)
Async XLA Ops:
  7.2 14.2 %copy-start.9 = (s32[16]{0:T(128)S(1)}, s32[16]{0:T(128)}, u32[]{:S(2)}) copy-start(s32[16]{0:T(128)} %param.31) | copy-start | bytes 196
  7.2 14.3 %copy-start.6 = (s32[2]{0:T(128)S(1)}, s32[2]{0:T(128)}, u32[]{:S(2)}) copy-start(s32[2]{0:T(128)} %param.33) | copy-start | bytes 28
  7.2 89.0 %all-gather.11.cloned.1.call-start = ((), (), s32[]{:S(2)}) async-start(), calls=%async_computation.4 | async-start | bytes 7077888 | tf_op jit(solution)/shard_map/all_gather | solution.py:43
  7.9 408.3 %all-gather.13.cloned.1.call-start = ((), (), s32[]{:S(2)}) async-start(), calls=%async_computation.5 | async-start | bytes 2359296 | tf_op jit(solution)/shard_map/all_gather | solution.py:52
  21.5 12.6 %copy-start.7 = (s32[2]{0:T(128)}, s32[2]{0:T(128)S(1)}, u32[]{:S(2)}) copy-start(s32[2]{0:T(128)S(1)} %get-tuple-element.494) | copy-start | bytes 28
  76.6 19.5 %copy-start.4 = (bf16[2,2048]{1,0:T(2,128)(2,1)S(1)}, bf16[2,2048]{1,0:T(2,128)(2,1)}, u32[]{:S(2)}) copy-start(bf16[2,2048]{1,0:T(2,128)(2,1)} %param.21) | copy-start | bytes 24580
  76.6 19.6 %copy-start.10 = (f32[2048]{0:T(1024)S(1)}, f32[2048]{0:T(1024)}, u32[]{:S(2)}) copy-start(f32[2048]{0:T(1024)} %param.22) | copy-start | bytes 24580
  107.5 11.9 all-to-all-start.2
  119.4 140.7 %all-to-all-start = ((bf16[3,8,128,512]{3,2,0,1:T(8,128)(2,1)}), bf16[3,8,128,512]{3,2,0,1:T(8,128)(2,1)S(1)}, u32[]{:S(2)}, u32[]{:S(2)}) async-start(bf16[3,8,128,512]{3,2,0,1:T(8,128)(2,1)} %select_bitcast_fusion), calls=%async_computation | async-start | bytes 6291456 | tf_op jit(solution)/shard_map/all_to_all | solution.py:142
  192.5 66.8 %copy-start.8 = (s32[2]{0:T(128)S(1)}, s32[2]{0:T(128)}, u32[]{:S(2)}) copy-start(s32[2]{0:T(128)} %copy-done.7) | copy-start | bytes 28
  260.0 135.7 %all-to-all-start.3 = ((bf16[8,2,512]{2,1,0:T(2,128)(2,1)}), bf16[8,2,512]{2,1,0:T(2,128)(2,1)}, u32[]{:S(2)}, u32[]{:S(2)}) async-start(bf16[8,2,512]{2,1,0:T(2,128)(2,1)} %reshape.531), calls=%async_computation.3 | async-start | bytes 32768 | tf_op jit(solution)/shard_map/all_to_all | solution.py:185
  275.0 9.9 copy-start
  298.4 14.3 %copy-start.3 = (bf16[1024,8,64]{0,2,1:T(8,128)(2,1)S(1)}, bf16[1024,8,64]{0,2,1:T(8,128)(2,1)}, u32[]{:S(2)}) copy-start(bf16[1024,8,64]{0,2,1:T(8,128)(2,1)} %reshape_squeeze.8) | copy-start | bytes 3145732
  335.6 3.9 copy-start.1
  343.4 1.3 copy-start.2
  351.4 3.9 copy-start.1
  359.2 1.3 copy-start.2
  367.1 3.9 copy-start.1
  375.0 1.3 copy-start.2
  382.9 3.9 copy-start.1
  390.8 1.3 copy-start.2
  392.1 7.9 copy-start.12
  395.7 19.6 %all-to-all-start.1 = ((bf16[8,128,512]{2,1,0:T(8,128)(2,1)}), bf16[8,128,512]{2,1,0:T(8,128)(2,1)S(1)}, u32[]{:S(2)}, u32[]{:S(2)}) async-start(bf16[8,128,512]{2,1,0:T(8,128)(2,1)} %copy.64), calls=%async_computation.1 | async-start | bytes 2097152 | tf_op jit(solution)/shard_map/all_to_all | solution.py:184
  399.9 311.8 %all-gather.19.cloned.1.call-start = ((), (), s32[]{:S(2)}) async-start(), calls=%async_computation.8 | async-start | bytes 21135360 | tf_op jit(solution)/shard_map/all_gather | solution.py:14
  422.2 383.5 %all-gather.15.cloned.1.call-start = ((), (), s32[]{:S(2)}) async-start(), calls=%async_computation.6 | async-start | bytes 18874368 | tf_op jit(solution)/shard_map/all_gather | solution.py:43
  422.8 439.1 %all-gather.17.cloned.1.call-start = ((), (), s32[]{:S(2)}) async-start(), calls=%async_computation.7 | async-start | bytes 9437184 | tf_op jit(solution)/shard_map/all_gather | solution.py:52
  423.3 301.0 %copy-start.5 = (bf16[2,2048]{1,0:T(2,128)(2,1)S(1)}, bf16[2,2048]{1,0:T(2,128)(2,1)}, u32[]{:S(2)}) copy-start(bf16[2,2048]{1,0:T(2,128)(2,1)} %param.21) | copy-start | bytes 24580
  423.4 746.9 %all-gather.21.cloned.1.call-start = ((), (), s32[]{:S(2)}) async-start(), calls=%async_computation.9 | async-start | bytes 21135360 | tf_op jit(solution)/shard_map/all_gather | solution.py:14
  724.3 81.4 %copy-start.11 = (f32[2048]{0:T(1024)S(1)}, f32[2048]{0:T(1024)}, u32[]{:S(2)}) copy-start(f32[2048]{0:T(1024)} %param.23) | copy-start | bytes 24580
Sparse Core Ops, SparseCore 0:
  9.9 49.3 all-gather.10
  61.2 27.9 all-gather.12
  422.3 289.3 all-gather.18
  713.5 92.1 all-gather.14
  807.4 54.3 all-gather.16
  879.7 290.4 all-gather.20
